TPU v7x, 32 devices: a whole 2x2x4 slice. The times are simulated.
32 devices in a mesh: mode: 16 (over z, y, x), real: 2 (over core).
Axes of the slice: x: 2, y: 2, z: 4, core: 2. Of those that a mesh axis runs over, the one named last changes fastest.
Arguments:
- input_field: bfloat16 [2, 2, 256, 16384], P(None, 'real', 'mode'), may hold values from -6 to 6
- kerr_coeff: bfloat16 [16, 64, 64], P('mode'), may hold values from -0.375 to 0.375
- block_list: int32 [16, 4], P('mode'), may hold values from 0 to 31
Outputs:
- density: float32 [512, 2, 256, 256], P('mode', None, 'real')
All inputs are finite; a program needn't handle non-finite values.
Results may differ from a plain program's by a relative error of at most 0.0085.
Values may be sent and summed in bfloat16 or wider, within the bound.
A program may use at most 64 MiB of HBM per device.

v0:
```python
import math

import jax
import jax.numpy as jnp
from jax import lax
from jax.sharding import PartitionSpec as P

MB = 8
FT = 128
NT = 16384
FB = 32


kerr_strength = 0.25


def kerr_terms(field_blocks, coeff_group, block_group):
    mode_l = jnp.take(field_blocks, block_group[:, 1], axis=2).astype(jnp.float32)
    mode_m = jnp.take(field_blocks, block_group[:, 2], axis=2).astype(jnp.float32)
    mode_n = jnp.take(field_blocks, block_group[:, 3], axis=2).astype(jnp.float32)
    realiz = field_blocks.shape[1]
    group_size = block_group.shape[0]
    steps_local = field_blocks.shape[4]
    prod_re = (
        mode_m[0][:, :, :, None, :] * mode_n[0][:, :, None, :, :]
        + mode_m[1][:, :, :, None, :] * mode_n[1][:, :, None, :, :]
    )
    prod_im = (
        mode_m[1][:, :, :, None, :] * mode_n[0][:, :, None, :, :]
        - mode_m[0][:, :, :, None, :] * mode_n[1][:, :, None, :, :]
    )
    pairs = (
        jnp.stack([prod_re, prod_im])
        .reshape(2, realiz, group_size, MB * MB, steps_local)
        .astype(jnp.bfloat16)
    )
    weighted = jnp.einsum(
        "kab,crkbt->crkat", coeff_group, pairs, preferred_element_type=jnp.float32
    )
    weighted = weighted.reshape(2, realiz, group_size, MB, MB, steps_local)
    term_re = jnp.sum(
        weighted[0] * mode_l[0][:, :, None] - weighted[1] * mode_l[1][:, :, None], axis=3
    )
    term_im = jnp.sum(
        weighted[0] * mode_l[1][:, :, None] + weighted[1] * mode_l[0][:, :, None], axis=3
    )
    one_hot = (
        block_group[:, 0][:, None] == jnp.arange(field_blocks.shape[2], dtype=jnp.int32)[None, :]
    ).astype(jnp.float32)
    return jnp.einsum(
        "kg,crkpt->crgpt", one_hot, jnp.stack([term_re, term_im]), precision=lax.Precision.HIGHEST
    )


def phase_table(extent, modulus):
    index_a = jnp.arange(extent, dtype=jnp.int32)[:, None]
    index_b = jnp.arange(extent, dtype=jnp.int32)[None, :]
    angle = 2.0 * math.pi / modulus * (index_a * index_b % modulus).astype(jnp.float32)
    return (jnp.cos(angle), -jnp.sin(angle))


def first_pass(table, data):
    table_high = table.astype(jnp.bfloat16)
    table_low = (table - table_high.astype(jnp.float32)).astype(jnp.bfloat16)
    upper = jnp.einsum("kn,rmnj->rmkj", table_high, data, preferred_element_type=jnp.float32)
    return upper + jnp.einsum("kn,rmnj->rmkj", table_low, data, preferred_element_type=jnp.float32)


def second_pass(table, data):
    return jnp.einsum("jn,rmkn->rmjk", table, data, precision=lax.Precision.HIGH)


def transform(by_mode):
    realiz = by_mode.shape[1]
    local_modes = by_mode.shape[2]
    signal = by_mode.reshape(2, realiz, local_modes, FT, FT)
    four_re, four_im = phase_table(FT, FT)
    twist_re, twist_im = phase_table(FT, NT)
    half_re = first_pass(four_re, signal[0]) - first_pass(four_im, signal[1])
    half_im = first_pass(four_re, signal[1]) + first_pass(four_im, signal[0])
    turned_re = half_re * twist_re - half_im * twist_im
    turned_im = half_re * twist_im + half_im * twist_re
    out_re = (second_pass(four_re, turned_re) - second_pass(four_im, turned_im)) / FT
    out_im = (second_pass(four_re, turned_im) + second_pass(four_im, turned_re)) / FT
    return jnp.stack([out_re, out_im]).astype(jnp.bfloat16)


def gram_parts(rows_part, cols_part):
    quarters = jnp.einsum(
        "crpbf,drqbf->bcdpq", rows_part, cols_part, preferred_element_type=jnp.float32
    )
    return jnp.stack(
        [quarters[:, 0, 0] + quarters[:, 1, 1], quarters[:, 1, 0] - quarters[:, 0, 1]], axis=1
    )


def shards(input_field, kerr_coeff, block_list):
    timed = lax.all_to_all(input_field, "mode", split_axis=3, concat_axis=2, tiled=True)
    realiz = timed.shape[1]
    width = timed.shape[2]
    steps_local = timed.shape[3]
    field_blocks = timed.reshape(2, realiz, width // MB, MB, steps_local)
    initial = jnp.zeros(field_blocks.shape, jnp.float32)
    running = initial
    coeff_piece = lax.all_gather(kerr_coeff, "mode", axis=0, tiled=True)
    block_piece = lax.all_gather(block_list, "mode", axis=0, tiled=True)
    block_count = block_piece.shape[0]
    coeff_groups = coeff_piece.reshape(
        block_count // 8, 8, coeff_piece.shape[1], coeff_piece.shape[2]
    )
    block_groups = block_piece.reshape(block_count // 8, 8, 4)

    def one_group(carried, groups):
        return (carried + kerr_terms(field_blocks, groups[0], groups[1]), None)

    running, unused = lax.scan(one_group, running, (coeff_groups, block_groups))
    kerr_sum = running
    kerr_sum = kerr_sum.reshape(2, realiz, width, steps_local)
    base = timed.astype(jnp.float32)
    stepped = jnp.stack(
        [base[0] - kerr_strength * kerr_sum[1], base[1] + kerr_strength * kerr_sum[0]]
    ).astype(jnp.bfloat16)
    by_mode = lax.all_to_all(stepped, "mode", split_axis=2, concat_axis=3, tiled=True)
    spectrum = transform(by_mode)
    banded = lax.all_to_all(spectrum, "mode", split_axis=3, concat_axis=2, tiled=True)
    bands_dev = banded.shape[3] * FT // FB
    spec_bands = banded.reshape(2, realiz, width, bands_dev, FB)
    scale = 1.0 / (FB * realiz * lax.axis_size("real"))
    row_count = width // lax.axis_size("real")
    row_first = lax.axis_index("real") * row_count
    shard_piece = lax.all_gather(spec_bands, "real", axis=1, tiled=True)
    own_part = lax.dynamic_slice_in_dim(shard_piece, row_first, row_count, 2)
    return gram_parts(own_part, shard_piece) * scale


def solution(mesh):
    return jax.shard_map(
        shards,
        mesh=mesh,
        in_specs=(P(None, "real", "mode", None), P("mode", None, None), P("mode", None)),
        out_specs=P("mode", None, "real", None),
        check_vma=False,
    )
```

profile of v0, /device:TPU:0, one launch (start us, length us, event | category | flops | bytes accessed | tf_op | source)
XLA Modules:
  0.0 297.2 jit_solution(920240638021889750)
XLA Ops:
  6.5 15.9 %copy.145 = bf16[2,1,16,16384]{2,0,1,3:T(2,128)(2,1)} copy(bf16[2,1,16,16384]{3,2,1,0:T(8,128)(2,1)} %param.7) | data formatting | bytes 2097152 | tf_op args[0]
  22.5 11.2 %reshape.574 = bf16[16,2,16384]{2,1,0:T(2,128)(2,1)} reshape(bf16[16384,1,2,16]{3,2,1,0:T(2,128)(2,1)} %bitcast.267) | data formatting | bytes 2097152
  33.7 8.5 %all-to-all-start = ((bf16[16,2,16384]{2,1,0:T(2,128)(2,1)}), bf16[16,2,16384]{2,1,0:T(2,128)(2,1)S(1)}, u32[]{:S(2)}, u32[]{:S(2)}) async-start(bf16[16,2,16384]{2,1,0:T(2,128)(2,1)} %reshape.574), calls=%async_computation | async-start | bytes 2097152 | tf_op jit(solution)/shard_map/all_to_all | solution.py:98
  42.2 50.9 %all-gather = s32[16,1,4]{2,1,0:T(1,128)S(1)} all-gather(s32[1,1,4]{2,1,0:T(1,128)S(1)} %bitcast.278), channel_id=1, replica_groups=mesh['mode'=16,'real'=2] {'mode'}, dimensions={0}, use_global_device_ids=true | all-gather | bytes 272 | tf_op jit(solution)/shard_map/all_gather | solution.py:106
  93.2 38.7 %all_gather.10 = bf16[16,64,64]{2,1,0:T(8,128)(2,1)S(1)} all-gather(bf16[1,64,64]{2,1,0:T(8,128)(2,1)S(1)} %copy-done.4), channel_id=1, replica_groups=mesh['mode'=16,'real'=2] {'mode'}, dimensions={0}, use_global_device_ids=true | all-gather | bytes 139264 | tf_op jit(solution)/shard_map/all_gather | solution.py:105
  131.8 7.4 %reshape.575 = bf16[16384,1,2,16]{3,2,1,0:T(2,128)(2,1)} reshape(bf16[16,2,16384]{2,1,0:T(2,128)(2,1)S(1)} %all-to-all-done) | data formatting | bytes 2097152
  139.2 17.7 %copy.200 = bf16[2,1,16,16,1024]{4,2,3,0,1:T(8,128)(2,1)S(1)} copy(bf16[2,1,16,16,1024]{2,0,4,3,1:T(2,128)(2,1)} %bitcast.265) | data formatting | bytes 2097152 | tf_op jit(solution)/shard_map/all_to_all | solution.py:98
  156.9 12.7 %copy.197 = bf16[2,1,16,16,1024]{4,3,2,0,1:T(8,128)(2,1)} copy(bf16[2,1,16,16,1024]{2,0,4,3,1:T(2,128)(2,1)} %bitcast.266) | data formatting | bytes 2097152 | tf_op jit(solution)/shard_map/all_to_all | solution.py:98
  169.6 23.4 %while.11 = (s32[]{:T(128)}, f32[2,1,32,8,1024]{4,2,3,0,1:T(8,128)S(1)}, s32[2,8,4]{1,2,0:T(4,128)S(1)}, bf16[2,1,32,8,1024]{4,3,2,1,0:T(8,128)(2,1)S(1)}, bf16[...) while((s32[]{:T(128)}, f32[2,1,32,8,1024]{4,2,3,0,1:T(8,128)S(1)}, ...), condition=%wide.region_3.5_spmd.clone, body=%wide.region_0.4_spmd.clone.sunk | while | flops 198970768 | bytes 36058028 | solution.py:116
  169.7 0.9 copy-done
  170.6 1.8 gather_fusion.2
  172.4 1.8 gather_fusion.1
  174.2 1.8 gather_fusion
  176.4 0.6 fusion.157
  177.0 0.7 convolution_bitcast_fusion.3
  177.7 1.5 subtract_reduce_fusion.2
  179.6 1.7 bitcast_add_fusion.2
  181.4 0.9 copy-done
  182.3 1.8 gather_fusion.2
  184.1 1.8 gather_fusion.1
  185.9 1.8 gather_fusion
  188.1 0.6 fusion.157
  188.8 0.7 convolution_bitcast_fusion.3
  189.5 1.5 subtract_reduce_fusion.2
  191.4 1.7 bitcast_add_fusion.2
  193.1 1.2 copy.152
  194.8 0.6 copy.147
  195.4 0.6 copy.153
  196.7 2.0 copy.155
  198.7 3.7 %all-to-all-start.1 = ((bf16[2,1,256,1024]{3,0,1,2:T(2,128)(2,1)}), bf16[2,1,256,1024]{3,0,1,2:T(2,128)(2,1)S(1)}, u32[]{:S(2)}, u32[]{:S(2)}) async-start(bf16[2,1,256,1024]{3,0,1,2:T(2,128)(2,1)} %copy.155), calls=%async_computation.1 | async-start | bytes 2097152 | tf_op jit(solution)/shard_map/all_to_all | solution.py:123
  203.3 14.6 %all-to-all-done.1 = bf16[2,1,256,1024]{3,0,1,2:T(2,128)(2,1)S(1)} async-done(((bf16[2,1,256,1024]{3,0,1,2:T(2,128)(2,1)}), bf16[2,1,256,1024]{3,0,1,2:T(2,128)(2,1)S(1)}, u32[]{:S(2)}, u32[]{:S(2)}) %all-to-all-start.1) | async-done | bytes 1048608 | tf_op jit(solution)/shard_map/all_to_all | solution.py:123
  218.2 0.9 fusion.137
  220.7 1.1 copy.157
  221.8 1.3 reshape.509
  226.4 1.2 fusion.39
  227.6 1.2 fusion.43
  228.8 1.2 fusion.30
  229.9 1.2 fusion.31
  231.2 1.0 copy.173
  232.2 21.6 %all_to_all.45 = bf16[2,1,16,128,128]{4,2,1,0,3:T(8,128)(2,1)S(1)} all-to-all(bf16[2,1,16,128,128]{4,2,1,0,3:T(8,128)(2,1)S(1)} %copy.173), channel_id=1, replica_groups=mesh['mode'=16,'real'=2] {'mode'}, dimensions={3} | all-to-all | bytes 2097152 | tf_op jit(solution)/shard_map/all_to_all | solution.py:125
  254.5 3.2 %reshape.513 = bf16[2,1,256,32,32]{4,3,2,0,1:T(8,128)(2,1)} reshape(bf16[2,1,16,16,8,128]{5,4,3,2,0,1:T(8,128)(2,1)S(1)} %copy.175) | data formatting | bytes 2097152 | tf_op jit(solution)/shard_map/reshape | solution.py:127
  257.7 5.2 %copy.176 = bf16[2,1,256,32,32]{2,4,1,0,3:T(8,128)(2,1)} copy(bf16[2,1,256,32,32]{4,3,2,0,1:T(8,128)(2,1)} %reshape.513) | data formatting | bytes 2097152 | tf_op jit(solution)/shard_map/reshape | solution.py:127
  263.0 9.0 %all-gather.3.cloned.1.call-done = bf16[2,2,256,32,32]{2,4,1,0,3:T(8,128)(2,1)} async-done(((bf16[2,1,256,32,32]{2,4,1,0,3:T(8,128)(2,1)}), bf16[2,2,256,32,32]{2,4,1,0,3:T(8,128)(2,1)}) %all-gather.3.cloned.1.call-update) | async-done | bytes 2097168 | tf_op jit(solution)/shard_map/all_gather | solution.py:131
  272.0 4.2 %convolution_bitcast_fusion.1 = f32[32,2,2,128,256]{3,4,1,2,0:T(8,128)S(1)} fusion(bf16[2,2,256,32,32]{2,4,1,0,3:T(8,128)(2,1)} %all-gather.3.cloned.1.call-done, s32[]{:T(128)S(6)} %select_n.66), kind=kOutput, calls=%fused_computation.52 | convolution fusion | flops 536870912 | bytes 19922948 | tf_op jit(solution)/shard_map/crpbf,drqbf->bcdpq/dot_general | solution.py:89
  276.2 0.6 fusion.18
  276.9 0.6 fusion.20
  277.5 3.9 %maximum_multiply_fusion = f32[32,2,128,256]{2,3,0,1:T(8,128)} fusion(f32[32,1,128,256]{2,3,0,1:T(8,128)S(1)} %fusion.18, f32[32,1,128,256]{2,3,0,1:T(8,128)S(1)} %fusion.20), kind=kLoop, calls=%fused_computation.53 | loop fusion | flops 4194304 | bytes 16777216 | tf_op jit(solution)/shard_map/mul | solution.py:133
  281.4 8.9 %copy.179 = f32[32,2,128,256]{3,2,1,0:T(8,128)} copy(f32[32,2,128,256]{2,3,0,1:T(8,128)} %maximum_multiply_fusion) | data formatting | bytes 16777216 | tf_op jit(solution)/shard_map/mul | solution.py:133
  (67 shorter events, 9.4 us)
Async XLA Ops:
  33.7 8.5 %copy-start.5 = (s32[1,4]{1,0:T(1,128)S(1)}, s32[1,4]{1,0:T(1,128)}, u32[]{:S(2)}) copy-start(s32[1,4]{1,0:T(1,128)} %param.9) | copy-start | bytes 52
  33.7 59.5 %copy-start.4 = (bf16[1,64,64]{2,1,0:T(8,128)(2,1)S(1)}, bf16[1,64,64]{2,1,0:T(8,128)(2,1)}, u32[]{:S(2)}) copy-start(bf16[1,64,64]{2,1,0:T(8,128)(2,1)} %param.8) | copy-start | bytes 24580
  33.7 98.1 %all-to-all-start = ((bf16[16,2,16384]{2,1,0:T(2,128)(2,1)}), bf16[16,2,16384]{2,1,0:T(2,128)(2,1)S(1)}, u32[]{:S(2)}, u32[]{:S(2)}) async-start(bf16[16,2,16384]{2,1,0:T(2,128)(2,1)} %reshape.574), calls=%async_computation | async-start | bytes 2097152 | tf_op jit(solution)/shard_map/all_to_all | solution.py:98
  169.6 1.0 copy-start
  179.6 1.7 copy-start.1
  181.4 1.0 copy-start
  191.3 1.7 copy-start.1
  193.1 1.2 copy-start.2
  198.7 19.2 %all-to-all-start.1 = ((bf16[2,1,256,1024]{3,0,1,2:T(2,128)(2,1)}), bf16[2,1,256,1024]{3,0,1,2:T(2,128)(2,1)S(1)}, u32[]{:S(2)}, u32[]{:S(2)}) async-start(bf16[2,1,256,1024]{3,0,1,2:T(2,128)(2,1)} %copy.155), calls=%async_computation.1 | async-start | bytes 2097152 | tf_op jit(solution)/shard_map/all_to_all | solution.py:123
  202.4 69.6 %all-gather.3.cloned.1.call-start = ((), (), s32[]{:S(2)}) async-start(), calls=%async_computation.3 | async-start | bytes 3145728 | tf_op jit(solution)/shard_map/all_gather | solution.py:131
  219.6 1.1 copy-start.3
Sparse Core Ops, SparseCore 0:
  263.1 8.8 all-gather.2
where the time goes:
time: 300 us; the launch traced here: 297 us
  blocking collectives  111 us (37%)
  local copies, waits for them, and re-layouts  106 us (35%)
  waiting for transfers between devices  23.6 us (8%)
  matrix products  18.1 us (6%)
  between operations  13.7 us (5%)
  starting transfers between devices  12.3 us (4%)
  other arithmetic  11.5 us (4%)
    all_gather x1, blocking collectives, shards(): block_piece = lax.all_gather(block_list, 'mode', axis=0, tiled=True)  50.9 us
    all_gather x1, blocking collectives, shards(): coeff_piece = lax.all_gather(kerr_coeff, 'mode', axis=0, tiled=True)  38.7 us
    unnamed x12, local copies, waits for them, and re-layouts  34.7 us
    all_to_all x2, local copies, waits for them, and re-layouts, shards(): lax.all_to_all(input_field, 'mode', split_axis=3, concat_axis=2, tiled=True)  30.4 us
    all_to_all x1, blocking collectives, shards(): lax.all_to_all(spectrum, 'mode', split_axis=3, concat_axis=2, tiled=True)  21.6 us
    all_to_all x1, waiting for transfers between devices, shards(): lax.all_to_all(stepped, 'mode', split_axis=2, concat_axis=3, tiled=True)  14.6 us
    all_gather x1, waiting for transfers between devices, shards(): shard_piece = lax.all_gather(spec_bands, 'real', axis=1, tiled=True)  9 us
    mul x1, local copies, waits for them, and re-layouts, shards(): return gram_parts(own_part, shard_piece) * scale  8.94 us
  transfers between devices with their start and end apart: 3, of which 2 were waited for; matrix products, arithmetic and copies ran while one was open for 0% of the time, Pallas kernels for 0%

commit v1 on v0

--- a/solution.py
+++ b/solution.py
@@ -1,8 +1,12 @@
+import functools
 import math
 
 import jax
 import jax.numpy as jnp
+import numpy as np
 from jax import lax
+from jax.experimental import pallas as pl
+from jax.experimental.pallas import tpu as pltpu
 from jax.sharding import PartitionSpec as P
 
 MB = 8
@@ -133,9 +137,291 @@
     return gram_parts(own_part, shard_piece) * scale
 
 
+VMEM = pltpu.VMEM
+BIG = 60 * 1024 * 1024
+
+
+def spread_kernel(parts, x_ref, coef_ref, list_ref, x_out, coef_out, list_out, sends, recvs, own):
+    me = lax.axis_index("mode")
+    steps = x_ref.shape[2] // parts
+    barrier = pltpu.get_barrier_semaphore()
+    for step in range(1, parts):
+        pl.semaphore_signal(
+            barrier,
+            inc=1,
+            device_id={"mode": lax.rem(me + step, parts)},
+            device_id_type=pl.DeviceIdType.MESH,
+        )
+    pl.semaphore_wait(barrier, parts - 1)
+    copies = []
+    for step in range(1, parts):
+        to = lax.rem(me + step, parts)
+        chunk = pl.ds(pl.multiple_of(to * steps, 128), steps)
+        pairs = (
+            (coef_ref, coef_out.at[me]),
+            (list_ref, list_out.at[me]),
+            (x_ref.at[:, :, chunk], x_out.at[me]),
+        )
+        for slot, (here, there) in enumerate(pairs):
+            copy = pltpu.make_async_remote_copy(
+                src_ref=here,
+                dst_ref=there,
+                send_sem=sends.at[step, slot],
+                recv_sem=recvs.at[step, slot],
+                device_id={"mode": to},
+                device_id_type=pl.DeviceIdType.MESH,
+            )
+            copy.start()
+            copies.append(copy)
+    chunk = pl.ds(pl.multiple_of(me * steps, 128), steps)
+    pairs = (
+        (coef_ref, coef_out.at[me]),
+        (list_ref, list_out.at[me]),
+        (x_ref.at[:, :, chunk], x_out.at[me]),
+    )
+    for slot, (here, there) in enumerate(pairs):
+        copy = pltpu.make_async_copy(here, there, own.at[slot])
+        copy.start()
+        copies.append(copy)
+    for copy in copies:
+        copy.wait()
+
+
+def spread(field, coef, listed, parts):
+    two, modes, times = field.shape
+    return pl.pallas_call(
+        functools.partial(spread_kernel, parts),
+        out_shape=(
+            jax.ShapeDtypeStruct((parts, two, modes, times // parts), field.dtype),
+            jax.ShapeDtypeStruct((parts,) + coef.shape, coef.dtype),
+            jax.ShapeDtypeStruct((parts,) + listed.shape, listed.dtype),
+        ),
+        in_specs=[pl.BlockSpec(memory_space=VMEM)] * 3,
+        out_specs=(pl.BlockSpec(memory_space=VMEM),) * 3,
+        scratch_shapes=[
+            pltpu.SemaphoreType.DMA((parts, 3)),
+            pltpu.SemaphoreType.DMA((parts, 3)),
+            pltpu.SemaphoreType.DMA((3,)),
+        ],
+        compiler_params=pltpu.CompilerParams(collective_id=0, has_side_effects=True),
+    )(field, coef, listed)
+
+
+def kerr_kernel(list_ref, field_ref, coef_ref, out_ref, fld, acc, rows):
+    parts, _, modes, steps = field_ref.shape
+    groups = fld.shape[1]
+    blocks = coef_ref.shape[0]
+    fine = steps // FT
+    piece = min(steps, 256)
+    for c in range(2):
+        fld[c] = field_ref[:, c].astype(jnp.float32).reshape(groups, MB, steps)
+    acc[...] = jnp.zeros_like(acc)
+
+    def one_block(k, carry):
+        to, bl, bm, bn = (list_ref[k, i] for i in range(4))
+        coef = coef_ref[k]
+        for first in range(0, steps, piece):
+            span = pl.ds(first, piece)
+            m_re, m_im = fld[0, bm, :, span][:, None], fld[1, bm, :, span][:, None]
+            n_re, n_im = fld[0, bn, :, span][None], fld[1, bn, :, span][None]
+            p_re = (m_re * n_re + m_im * n_im).reshape(MB * MB, piece)
+            p_im = (m_im * n_re - m_re * n_im).reshape(MB * MB, piece)
+            pairs = jnp.concatenate([p_re, p_im], axis=1).astype(jnp.bfloat16)
+            w = jnp.dot(coef, pairs, preferred_element_type=jnp.float32)
+            w_re = w[:, :piece].reshape(MB, MB, piece)
+            w_im = w[:, piece:].reshape(MB, MB, piece)
+            l_re, l_im = fld[0, bl, :, span][:, None], fld[1, bl, :, span][:, None]
+            acc[0, to, :, span] += jnp.sum(w_re * l_re - w_im * l_im, axis=0)
+            acc[1, to, :, span] += jnp.sum(w_re * l_im + w_im * l_re, axis=0)
+        return carry
+
+    lax.fori_loop(0, blocks, one_block, 0)
+
+    def one_group(g, carry):
+        new = (
+            fld[0, g] - kerr_strength * acc[1, g],
+            fld[1, g] + kerr_strength * acc[0, g],
+        )
+        for c in range(2):
+            for n in range(fine):
+                at = pl.ds(g * (MB * 2 * fine) + c * fine + n, MB, stride=2 * fine)
+                rows[at, :] = new[c][:, n * FT : (n + 1) * FT]
+        return carry
+
+    lax.fori_loop(0, groups, one_group, 0)
+    out_ref[...] = rows[...].astype(jnp.bfloat16)
+
+
+def kerr_step(listed, timed, coef):
+    parts, _, modes, steps = timed.shape
+    width = parts * modes
+    count = width * 2 * steps // FT
+    return pl.pallas_call(
+        kerr_kernel,
+        out_shape=jax.ShapeDtypeStruct((count, FT), jnp.bfloat16),
+        in_specs=[
+            pl.BlockSpec(memory_space=pltpu.SMEM),
+            pl.BlockSpec(memory_space=VMEM),
+            pl.BlockSpec(memory_space=VMEM),
+        ],
+        out_specs=pl.BlockSpec(memory_space=VMEM),
+        scratch_shapes=[
+            VMEM((2, width // MB, MB, steps), jnp.float32),
+            VMEM((2, width // MB, MB, steps), jnp.float32),
+            VMEM((count, FT), jnp.float32),
+        ],
+        compiler_params=pltpu.CompilerParams(vmem_limit_bytes=BIG),
+    )(listed, timed, coef)
+
+
+def dft_tables(parts):
+    a = np.arange(FT)
+    four = np.exp(-2j * np.pi / FT * (np.outer(a, a) % FT))
+    twist = np.exp(-2j * np.pi / NT * (np.outer(a, a) % NT)) / FT
+    real = np.block([[four.real, -four.imag], [four.imag, four.real]])
+    first = real.reshape(2 * FT, 2, parts, FT // parts).transpose(0, 2, 1, 3)
+    first = first.reshape(2 * FT, 2 * FT)
+    second = real.reshape(2, FT, 2 * FT).transpose(1, 0, 2).reshape(2 * FT, 2 * FT)
+
+    def split(t):
+        t = t.astype(np.float32)
+        high = t.astype(jnp.bfloat16)
+        return high, (t - high.astype(np.float32)).astype(jnp.bfloat16)
+
+    return (
+        *split(first),
+        twist.real.astype(np.float32),
+        twist.imag.astype(np.float32),
+        *split(second),
+    )
+
+
+def dft_kernel(x_ref, f1h, f1l, tw_re, tw_im, f2h, f2l, out_ref, rows):
+    modes = x_ref.shape[1]
+    nt = (((1,), (1,)), ((), ()))
+    dot = functools.partial(jnp.dot, preferred_element_type=jnp.float32)
+    dot_nt = functools.partial(
+        lax.dot_general, dimension_numbers=nt, preferred_element_type=jnp.float32
+    )
+    for m in range(0, modes, 2):
+        x = jnp.concatenate(
+            [x_ref[:, m].reshape(2 * FT, FT), x_ref[:, m + 1].reshape(2 * FT, FT)], axis=1
+        )
+        half = dot(f1h[...], x) + dot(f1l[...], x)
+        turned = []
+        for i in range(2):
+            h_re, h_im = half[:FT, i * FT : (i + 1) * FT], half[FT:, i * FT : (i + 1) * FT]
+            turned.append(
+                jnp.concatenate(
+                    [
+                        h_re * tw_re[...] - h_im * tw_im[...],
+                        h_re * tw_im[...] + h_im * tw_re[...],
+                    ],
+                    axis=1,
+                )
+            )
+        turned = jnp.concatenate(turned, axis=0)
+        high = turned.astype(jnp.bfloat16)
+        low = (turned - high.astype(jnp.float32)).astype(jnp.bfloat16)
+        out = dot_nt(f2h[...], high) + dot_nt(f2h[...], low) + dot_nt(f2l[...], high)
+        for i in range(2):
+            rows[pl.ds(m + i, 2 * FT, stride=modes), :] = out[:, i * FT : (i + 1) * FT]
+    out_ref[...] = rows[...].astype(jnp.bfloat16)
+
+
+def dft(by_mode):
+    parts, modes, _, _ = by_mode.shape
+    tables = dft_tables(parts)
+    return pl.pallas_call(
+        dft_kernel,
+        out_shape=jax.ShapeDtypeStruct((2 * FT * modes, FT), jnp.bfloat16),
+        in_specs=[pl.BlockSpec(memory_space=VMEM)] * 7,
+        out_specs=pl.BlockSpec(memory_space=VMEM),
+        scratch_shapes=[VMEM((2 * FT * modes, FT), jnp.float32)],
+        compiler_params=pltpu.CompilerParams(vmem_limit_bytes=BIG),
+    )(by_mode, *tables)
+
+
+def gram_kernel(scale, half_ref, *refs):
+    *spec_refs, out_ref = refs
+    parts, _, _, modes, _ = spec_refs[0].shape
+    row_count = out_ref.shape[2]
+    sources = row_count // modes
+    first = half_ref[0] * sources
+    cols, rows_re, rows_im = [], [], []
+    for ref in spec_refs:
+        re, im = (ref[:, 0, c].reshape(parts * modes, FT) for c in range(2))
+        own = pl.ds(first, sources)
+        own_re, own_im = (ref[own, 0, c].reshape(row_count, FT) for c in range(2))
+        cols += [re, im]
+        rows_re += [own_re, own_im]
+        rows_im += [own_im, -own_re]
+    cols = jnp.concatenate(cols, axis=1)
+    rows = jnp.concatenate(
+        [jnp.concatenate(rows_re, axis=1), jnp.concatenate(rows_im, axis=1)], axis=0
+    )
+    lane = lax.broadcasted_iota(jnp.int32, rows.shape, 1)
+    band = (lane % FT) // FB
+    for g in range(FT // FB):
+        kept = jnp.where(band == g, rows, jnp.zeros_like(rows))
+        out = lax.dot_general(
+            kept, cols, (((1,), (1,)), ((), ())), preferred_element_type=jnp.float32
+        )
+        out_ref[g] = (out * scale).reshape(2, row_count, parts * modes)
+
+
+def gram(half, spectra, row_count, scale):
+    parts, high, _, modes, _ = spectra[0].shape
+    width = parts * modes
+    per = FT // FB
+    return pl.pallas_call(
+        functools.partial(gram_kernel, scale),
+        grid=(high,),
+        out_shape=jax.ShapeDtypeStruct((high * per, 2, row_count, width), jnp.float32),
+        in_specs=[pl.BlockSpec(memory_space=pltpu.SMEM)]
+        + [pl.BlockSpec((parts, 1, 2, modes, FT), lambda j: (0, j, 0, 0, 0))] * len(spectra),
+        out_specs=pl.BlockSpec((per, 2, row_count, width), lambda j: (j, 0, 0, 0)),
+        compiler_params=pltpu.CompilerParams(vmem_limit_bytes=BIG),
+    )(half, *spectra)
+
+
+def tiled_shards(input_field, kerr_coeff, block_list):
+    parts, sides = lax.axis_size("mode"), lax.axis_size("real")
+    _, _, modes, times = input_field.shape
+    width = parts * modes
+    fine = FT // parts
+    coef = kerr_coeff[0].reshape(MB, MB, MB * MB).transpose(1, 0, 2).reshape(MB * MB, MB * MB)
+    listed = jnp.pad(block_list, ((0, 7), (0, FT - block_list.shape[1])))
+    timed, coefs, lists = spread(input_field.reshape(2, modes, times), coef, listed, parts)
+    stepped = kerr_step(lists[:, 0, :4], timed, coefs)
+    stepped = stepped.reshape(parts, modes, 2 * fine, FT)
+    by_mode = lax.all_to_all(stepped, "mode", split_axis=0, concat_axis=0)
+    spectrum = dft(by_mode).reshape(parts, fine, 2, modes, FT)
+    own = lax.all_to_all(spectrum, "mode", split_axis=0, concat_axis=0)
+    ring = [(i, (i + 1) % sides) for i in range(sides)]
+    spectra = [own]
+    for _ in range(sides - 1):
+        spectra.append(lax.ppermute(spectra[-1], "real", ring))
+    half = lax.axis_index("real").astype(jnp.int32).reshape(1)
+    return gram(half, spectra, width // sides, 1.0 / (FB * sides))
+
+
+def tiles_fit(mesh):
+    parts = mesh.shape["mode"]
+    return FT % parts == 0 and (2 * FT // parts) % 16 == 0 and mesh.shape["real"] <= 2
+
+
+def either(mesh, input_field, kerr_coeff, block_list):
+    modes = input_field.shape[2]
+    blocks_each = kerr_coeff.shape[0]
+    fits = tiles_fit(mesh) and modes % 16 == 0 and blocks_each == 1
+    fits = fits and input_field.shape[1] == 1 and input_field.shape[3] == NT
+    return (tiled_shards if fits else shards)(input_field, kerr_coeff, block_list)
+
+
 def solution(mesh):
     return jax.shard_map(
-        shards,
+        functools.partial(either, mesh),
         mesh=mesh,
         in_specs=(P(None, "real", "mode", None), P("mode", None, None), P("mode", None)),
         out_specs=P("mode", None, "real", None),

time: 300 us -> 132 us (0.44)
  local copies, waits for them, and re-layouts: 106 us -> 5.02 us
  Pallas kernels: 0 us -> 54 us
  blocking collectives: 111 us -> 69.8 us
  waiting for transfers between devices: 23.6 us -> 2.66 us
  matrix products: 18.1 us -> 0 us
  between operations: 13.7 us -> 0.02 us
  starting transfers between devices: 12.3 us -> 0.01 us
  other arithmetic: 11.5 us -> 0 us
    all_gather x2 -> x0, blocking collectives: 89.6 us -> none  [the longest x1 50.9 us: shards(): block_piece = lax.all_gather(block_list, 'mode', axis=0, tiled=True)]
    pallas_call x0 -> x4, Pallas kernels: none -> 54 us  [the longest x1 32.3 us: spread(): pl.pallas_call(functools.partial(spread_kernel, parts), out_shape=(jax.Sh...]
    all_to_all x1 -> x2, blocking collectives: 21.6 us -> 69.8 us  [the longest x1 40.2 us: tiled_shards(): by_mode = lax.all_to_all(stepped, 'mode', split_axis=0, concat_axis=0)]
    unnamed x12 -> x4, local copies, waits for them, and re-layouts: 34.7 us -> 1.02 us
    all_to_all x5 -> x0, local copies, waits for them, and re-layouts: 31.3 us -> none  [the longest x2 30.4 us: shards(): lax.all_to_all(input_field, 'mode', split_axis=3, concat_axis=2, tiled=True)]
    dot_general x17 -> x0, matrix products: 18.1 us -> none  [the longest x4 4.74 us: second_pass(): jnp.einsum('jn,rmkn->rmjk', table, data, precision=lax.Precision.HIGH)]
    all_to_all x2 -> x0, waiting for transfers between devices: 14.6 us -> none  [the longest x1 14.6 us: shards(): lax.all_to_all(stepped, 'mode', split_axis=2, concat_axis=3, tiled=True)]
    all_to_all x2 -> x0, starting transfers between devices: 12.1 us -> none  [the longest x1 8.47 us: shards(): lax.all_to_all(input_field, 'mode', split_axis=3, concat_axis=2, tiled=True)]
  transfers between devices with their start and end apart: 3 -> 1, of which waited for: 2 -> 1; matrix products, arithmetic and copies ran while one was open for 0% -> 0% of each run, Pallas kernels for 0% -> 0%
where the time goes in v1:
time: 132 us; the launch traced here: 131 us
  blocking collectives  69.8 us (53%)
  Pallas kernels  54 us (41%)
  local copies, waits for them, and re-layouts  5.02 us (4%)
  waiting for transfers between devices  2.66 us (2%)
    all_to_all x1, blocking collectives, tiled_shards(): by_mode = lax.all_to_all(stepped, 'mode', split_axis=0, concat_axis=0)  40.2 us
    pallas_call x1, Pallas kernels, spread(): pl.pallas_call(functools.partial(spread_kernel, parts), out_shape=(jax.Sh...  32.3 us
    all_to_all x1, blocking collectives, tiled_shards(): own = lax.all_to_all(spectrum, 'mode', split_axis=0, concat_axis=0)  29.6 us
    pallas_call x1, Pallas kernels, gram(): pl.pallas_call(functools.partial(gram_kernel, scale), grid=(high,), out_s...  8.57 us
    pallas_call x1, Pallas kernels, kerr_step(): pl.pallas_call(kerr_kernel, out_shape=jax.ShapeDtypeStruct((count, FT), j...  7.82 us
    pallas_call x1, Pallas kernels, dft(): pl.pallas_call(dft_kernel, out_shape=jax.ShapeDtypeStruct((2 * FT * modes...  5.28 us
    ppermute x1, waiting for transfers between devices, tiled_shards(): spectra.append(lax.ppermute(spectra[-1], 'real', ring))  2.66 us
  transfers between devices with their start and end apart: 1, of which 1 were waited for; matrix products, arithmetic and copies ran while one was open for 0% of the time, Pallas kernels for 0%

profile of v1, /device:TPU:0, one launch (start us, length us, event | category | flops | bytes accessed | tf_op | source)
XLA Modules:
  0.0 131.4 jit_solution(12285042042231162978)
XLA Ops:
  0.0 1.3 %copy.15 = bf16[8,8,64]{2,0,1:T(8,128)(2,1)} copy(bf16[8,8,64]{2,1,0:T(8,128)(2,1)} %bitcast.16) | data formatting | bytes 16384 | tf_op jit(solution)/shard_map/reshape;squeeze | solution.py:393
  1.3 1.2 pad.4.list_ref
  2.6 32.3 %shard_map.91 = (bf16[16,2,16,1024]{3,2,1,0:T(8,128)(2,1)}, bf16[16,64,64]{2,1,0:T(8,128)(2,1)}, s32[16,8,128]{2,1,0:T(8,128)}) custom-call(bf16[2,16,16384]{2,1,0:T(8,128)(2,1)} %bitcast.13, bf16[64,64]{1,0:T(8,128)(2,1)} %bitcast.14, s32[8,128]{1,0:T(8,128)} %pad.4.list_ref), custom_call_target="tpu_custom_call" | custom-call | tf_op jit(solution)/shard_map/pallas_call | solution.py:192
  34.9 1.4 %slice.3 = s32[16,1,4]{2,1,0:T(1,128)} slice(s32[16,8,128]{2,1,0:T(8,128)} %get-tuple-element.8), slice={[0:16], [0:1], [0:4]} | slice | bytes 512 | tf_op jit(solution)/shard_map/slice | solution.py:396
  36.3 7.8 %shard_map.92 = bf16[4096,128]{1,0:T(8,128)(2,1)} custom-call(s32[16,4]{1,0:T(8,128)} %bitcast.15, bf16[16,2,16,1024]{3,2,1,0:T(8,128)(2,1)} %get-tuple-element.9.field_ref, bf16[16,64,64]{2,1,0:T(8,128)(2,1)} %get-tuple-element.10.coef_ref), custom_call_target="tpu_custom_call" | custom-call | tf_op jit(solution)/shard_map/pallas_call | solution.py:259
  44.1 40.2 %all_to_all.10.x_ref = bf16[16,16,16,128]{3,2,1,0:T(8,128)(2,1)} all-to-all(bf16[16,16,16,128]{3,2,1,0:T(8,128)(2,1)} %bitcast.12), channel_id=1, replica_groups=mesh['mode'=16,'real'=2] {'mode'}, dimensions={0} | all-to-all | bytes 2097152 | tf_op jit(solution)/shard_map/all_to_all | solution.py:398
  84.3 5.3 %shard_map.93 = bf16[4096,128]{1,0:T(8,128)(2,1)} custom-call(bf16[16,16,16,128]{3,2,1,0:T(8,128)(2,1)} %all_to_all.10.x_ref, bf16[256,256]{1,0:T(8,128)(2,1)} %constant.18.clone.f1h, bf16[256,256]{1,0:T(8,128)(2,1)} %constant.19.clone.f1l, f32[128,128]{1,0:T(8,128)} %constant.20.clone.tw_re, f32[128,128]{1,0:T(8,128)} %constant.21.clone.tw_im, ...), custom_call_target="tpu_custom_call" | custom-call | tf_op jit(solution)/shard_map/pallas_call | solution.py:335
  89.6 29.6 %all_to_all.11.refs_0_ = bf16[16,8,2,16,128]{4,3,2,1,0:T(8,128)(2,1)S(1)} all-to-all(bf16[16,8,2,16,128]{4,3,2,1,0:T(8,128)(2,1)} %bitcast.11), channel_id=1, replica_groups=mesh['mode'=16,'real'=2] {'mode'}, dimensions={0} | all-to-all | bytes 2097152 | tf_op jit(solution)/shard_map/all_to_all | solution.py:400
  119.2 0.0 copy-start
  119.2 0.0 collective-permute-start
  119.2 2.7 %collective-permute-done.refs_1_ = bf16[16,8,2,16,128]{4,3,2,1,0:T(8,128)(2,1)S(1)} collective-permute-done((bf16[16,8,2,16,128]{4,3,2,1,0:T(8,128)(2,1)S(1)}, bf16[16,8,2,16,128]{4,3,2,1,0:T(8,128)(2,1)S(1)}, u32[]{:S(2)}, u32[]{:S(2)}) %collective-permute-start) | collective-permute-done | bytes 1048608 | tf_op jit(solution)/shard_map/ppermute | solution.py:404
  121.9 0.0 copy-start.1
  121.9 0.0 copy-done
  121.9 1.0 copy-done.1
  122.9 8.6 %shard_map.94 = f32[32,2,128,256]{3,2,1,0:T(8,128)} custom-call(s32[1]{0:T(128)} %bitcast.half_ref, bf16[16,8,2,16,128]{4,3,2,1,0:T(8,128)(2,1)} %copy-done, bf16[16,8,2,16,128]{4,3,2,1,0:T(8,128)(2,1)} %copy-done.1), custom_call_target="tpu_custom_call" | custom-call | tf_op jit(solution)/shard_map/pallas_call | solution.py:377
Async XLA Ops:
  119.2 2.7 %copy-start = (bf16[16,8,2,16,128]{4,3,2,1,0:T(8,128)(2,1)}, bf16[16,8,2,16,128]{4,3,2,1,0:T(8,128)(2,1)S(1)}, u32[]{:S(2)}) copy-start(bf16[16,8,2,16,128]{4,3,2,1,0:T(8,128)(2,1)S(1)} %all_to_all.11.refs_0_) | copy-start | bytes 3145732
  119.2 2.7 %collective-permute-start = (bf16[16,8,2,16,128]{4,3,2,1,0:T(8,128)(2,1)S(1)}, bf16[16,8,2,16,128]{4,3,2,1,0:T(8,128)(2,1)S(1)}, u32[]{:S(2)}, u32[]{:S(2)}) collective-permute-start(bf16[16,8,2,16,128]{4,3,2,1,0:T(8,128)(2,1)S(1)} %all_to_all.11.refs_0_), channel_id=1, source_target_pairs={{0,1},{1,0},{2,3},{3,2},{4,5},{5,4},{6,7},{7,6},{8,9},{9,8},{10,11... | collective-permute-start | bytes 3145736 | tf_op jit(solution)/shard_map/ppermute | solution.py:404
  121.9 1.0 copy-start.1

commit v2 on v0

--- a/solution.py
+++ b/solution.py
@@ -1,8 +1,12 @@
+import functools
 import math
 
 import jax
 import jax.numpy as jnp
+import numpy as np
 from jax import lax
+from jax.experimental import pallas as pl
+from jax.experimental.pallas import tpu as pltpu
 from jax.sharding import PartitionSpec as P
 
 MB = 8
@@ -133,9 +137,351 @@
     return gram_parts(own_part, shard_piece) * scale
 
 
+VMEM = pltpu.VMEM
+BIG = 60 * 1024 * 1024
+
+
+def step_order(parts):
+    return sorted(range(1, parts), key=lambda step: (-min(step, parts - step), step))
+
+
+def remote(here, there, sent, landed, target):
+    copy = pltpu.make_async_remote_copy(
+        src_ref=here,
+        dst_ref=there,
+        send_sem=sent,
+        recv_sem=landed,
+        device_id=target,
+        device_id_type=pl.DeviceIdType.MESH,
+    )
+    copy.start()
+    return copy
+
+
+def kerr_terms_at(first, piece, k, list_s, coef, fld, terms):
+    span = pl.ds(first, piece)
+    bl, bm, bn = (list_s[k, 0, i] for i in (1, 2, 3))
+    m_re, m_im = fld[0, bm, :, span][:, None], fld[1, bm, :, span][:, None]
+    n_re, n_im = fld[0, bn, :, span][None], fld[1, bn, :, span][None]
+    p_re = (m_re * n_re + m_im * n_im).reshape(MB * MB, piece)
+    p_im = (m_im * n_re - m_re * n_im).reshape(MB * MB, piece)
+    pairs = jnp.concatenate([p_re, p_im], axis=1).astype(jnp.bfloat16)
+    w = jnp.dot(coef, pairs, preferred_element_type=jnp.float32)
+    w_re = w[:, :piece].reshape(MB, MB, piece)
+    w_im = w[:, piece:].reshape(MB, MB, piece)
+    l_re, l_im = fld[0, bl, :, span][:, None], fld[1, bl, :, span][:, None]
+    at = pl.ds(pl.multiple_of(k * MB, MB), MB)
+    terms[0, at, span] = jnp.sum(w_re * l_re - w_im * l_im, axis=0)
+    terms[1, at, span] = jnp.sum(w_re * l_im + w_im * l_re, axis=0)
+
+
+def owner_table(blocks, width, list_s):
+    shape = (width, blocks * MB)
+    row = lax.broadcasted_iota(jnp.int32, shape, 0)
+    col = lax.broadcasted_iota(jnp.int32, shape, 1)
+    wanted = jnp.full(shape, -1, jnp.int32)
+    for k in range(blocks):
+        wanted = jnp.where(col // MB == k, list_s[k, 0, 0] * MB + col % MB, wanted)
+    return (row == wanted).astype(jnp.float32).astype(jnp.bfloat16)
+
+
+def whole_kernel(parts, sides, x_ref, coef_ref, list_ref, f1h, f1l, tw_re, tw_im, f2h, f2l,
+                 out_ref, timed, coefs, lists, list_s, fld, terms, rows, stepped, by_mode, spec,
+                 sends, recvs, own_sems):
+    me = lax.axis_index("mode")
+    other = {"real": 1 - lax.axis_index("real")}
+    _, modes, times = x_ref.shape
+    steps = times // parts
+    width = parts * modes
+    groups = width // MB
+    fine = steps // FT
+    half = steps // 2
+    piece = min(half, 256)
+    order = step_order(parts)
+    barrier = pltpu.get_barrier_semaphore()
+    for step in order:
+        to = {"mode": lax.rem(me + step, parts)}
+        pl.semaphore_signal(barrier, inc=1, device_id=to, device_id_type=pl.DeviceIdType.MESH)
+    if sides > 1:
+        pl.semaphore_signal(barrier, inc=1, device_id=other, device_id_type=pl.DeviceIdType.MESH)
+    pl.semaphore_wait(barrier, parts - 1 + (sides > 1))
+
+    def chunk(to, part):
+        at = pl.multiple_of(to * steps + part * half, 128)
+        return x_ref.at[:, :, pl.ds(at, half)]
+
+    def landing(part):
+        return timed.at[me, :, :, pl.ds(part * half, half)]
+
+    small, first, later = [], [], []
+    for step in order:
+        to = lax.rem(me + step, parts)
+        there = {"mode": to}
+        small.append(remote(coef_ref, coefs.at[me], sends.at[0, step], recvs.at[0, step], there))
+        small.append(remote(list_ref, lists.at[me], sends.at[1, step], recvs.at[1, step], there))
+    for part, copies in ((0, first), (1, later)):
+        for step in order:
+            to = lax.rem(me + step, parts)
+            copies.append(
+                remote(
+                    chunk(to, part),
+                    landing(part),
+                    sends.at[2 + part, step],
+                    recvs.at[2 + part, step],
+                    {"mode": to},
+                )
+            )
+    for slot, (here, there) in enumerate(
+        (
+            (coef_ref, coefs.at[me]),
+            (list_ref, lists.at[me]),
+            (chunk(me, 0), landing(0)),
+            (chunk(me, 1), landing(1)),
+        )
+    ):
+        copy = pltpu.make_async_copy(here, there, own_sems.at[slot])
+        copy.start()
+        (small, small, first, later)[slot].append(copy)
+    for copy in small:
+        copy.wait()
+    copy = pltpu.make_async_copy(lists, list_s, own_sems.at[4])
+    copy.start()
+    copy.wait()
+    blocks = coefs.shape[0]
+    owners = owner_table(blocks, width, list_s)
+    for part, copies in ((0, first), (1, later)):
+        for copy in copies:
+            copy.wait()
+        span = pl.ds(part * half, half)
+        for c in range(2):
+            fld[c, :, :, span] = timed[:, c, :, span].astype(jnp.float32).reshape(groups, MB, half)
+
+        def one_block(k, carry):
+            coef = coefs[k]
+            for at in range(part * half, (part + 1) * half, piece):
+                kerr_terms_at(at, piece, k, list_s, coef, fld, terms)
+            return carry
+
+        lax.fori_loop(0, blocks, one_block, 0)
+        for c in range(2):
+            term = terms[1 - c, :, span]
+            high = term.astype(jnp.bfloat16)
+            low = (term - high.astype(jnp.float32)).astype(jnp.bfloat16)
+            kerr = jnp.dot(owners, high, preferred_element_type=jnp.float32)
+            kerr = kerr + jnp.dot(owners, low, preferred_element_type=jnp.float32)
+            turn = kerr_strength * (2 * c - 1)
+            new = fld[c, :, :, span].reshape(width, half) + turn * kerr
+            for g in range(groups):
+                for n in range(half // FT):
+                    row = g * (MB * 2 * fine) + c * fine + part * (half // FT) + n
+                    rows[pl.ds(row, MB, stride=2 * fine), :] = new[
+                        g * MB : (g + 1) * MB, n * FT : (n + 1) * FT
+                    ]
+    stepped[...] = rows[...].astype(jnp.bfloat16).reshape(stepped.shape)
+
+    pending = []
+    for step in order:
+        to = lax.rem(me + step, parts)
+        pending.append(
+            remote(stepped.at[to], by_mode.at[me], sends.at[4, step], recvs.at[4, step], {"mode": to})
+        )
+    copy = pltpu.make_async_copy(stepped.at[me], by_mode.at[me], own_sems.at[5])
+    copy.start()
+    for copy in pending + [copy]:
+        copy.wait()
+
+    dft_kernel(by_mode, f1h, f1l, tw_re, tw_im, f2h, f2l, rows)
+    spec[...] = rows[...].astype(jnp.bfloat16).reshape(spec.shape)
+
+    pending, passed = [], []
+    for step in order:
+        to = lax.rem(me + step, parts)
+        pending.append(
+            (
+                remote(spec.at[to], out_ref.at[0, me], sends.at[5, step], recvs.at[5, step], {"mode": to}),
+                lax.rem(me - step + parts, parts),
+            )
+        )
+    copy = pltpu.make_async_copy(spec.at[me], out_ref.at[0, me], own_sems.at[6])
+    copy.start()
+    if sides > 1:
+        passed.append(remote(spec.at[me], out_ref.at[1, me], sends.at[6, 0], recvs.at[6, 0], other))
+    for step, (arrival, source) in zip(order, pending):
+        arrival.wait_recv()
+        if sides > 1:
+            passed.append(
+                remote(
+                    out_ref.at[0, source],
+                    out_ref.at[1, source],
+                    sends.at[6, step],
+                    recvs.at[6, step],
+                    other,
+                )
+            )
+    copy.wait()
+    for arrival, _ in pending:
+        arrival.wait_send()
+    for copy in passed:
+        copy.wait()
+
+
+def spectra_of(field, coef, listed, parts, sides):
+    _, modes, times = field.shape
+    steps = times // parts
+    width = parts * modes
+    fine = steps // FT
+    half = jnp.bfloat16
+    return pl.pallas_call(
+        functools.partial(whole_kernel, parts, sides),
+        out_shape=jax.ShapeDtypeStruct((sides, parts, fine, 2, modes, FT), half),
+        in_specs=[pl.BlockSpec(memory_space=VMEM)] * 9,
+        out_specs=pl.BlockSpec(memory_space=VMEM),
+        scratch_shapes=[
+            VMEM((parts, 2, modes, steps), half),
+            VMEM((parts,) + coef.shape, half),
+            VMEM((parts,) + listed.shape, jnp.int32),
+            pltpu.SMEM((parts,) + listed.shape, jnp.int32),
+            VMEM((2, width // MB, MB, steps), jnp.float32),
+            VMEM((2, parts * MB, steps), jnp.float32),
+            VMEM((2 * width * fine, FT), jnp.float32),
+            VMEM((parts, modes, 2 * fine, FT), half),
+            VMEM((parts, modes, 2 * fine, FT), half),
+            VMEM((parts, fine, 2, modes, FT), half),
+            pltpu.SemaphoreType.DMA((7, parts)),
+            pltpu.SemaphoreType.DMA((7, parts)),
+            pltpu.SemaphoreType.DMA((7,)),
+        ],
+        compiler_params=pltpu.CompilerParams(
+            collective_id=0, has_side_effects=True, vmem_limit_bytes=BIG
+        ),
+    )(field, coef, listed, *dft_tables(parts))
+
+
+def dft_tables(parts):
+    a = np.arange(FT)
+    four = np.exp(-2j * np.pi / FT * (np.outer(a, a) % FT))
+    twist = np.exp(-2j * np.pi / NT * (np.outer(a, a) % NT)) / FT
+    real = np.block([[four.real, -four.imag], [four.imag, four.real]])
+    first = real.reshape(2 * FT, 2, parts, FT // parts).transpose(0, 2, 1, 3)
+    first = first.reshape(2 * FT, 2 * FT)
+    second = real.reshape(2, FT, 2 * FT).transpose(1, 0, 2).reshape(2 * FT, 2 * FT)
+
+    def split(t):
+        t = t.astype(np.float32)
+        high = t.astype(jnp.bfloat16)
+        return high, (t - high.astype(np.float32)).astype(jnp.bfloat16)
+
+    return (
+        *split(first),
+        twist.real.astype(np.float32),
+        twist.imag.astype(np.float32),
+        *split(second),
+    )
+
+
+def dft_kernel(x_ref, f1h, f1l, tw_re, tw_im, f2h, f2l, rows):
+    modes = x_ref.shape[1]
+    nt = (((1,), (1,)), ((), ()))
+    dot = functools.partial(jnp.dot, preferred_element_type=jnp.float32)
+    dot_nt = functools.partial(
+        lax.dot_general, dimension_numbers=nt, preferred_element_type=jnp.float32
+    )
+    for m in range(0, modes, 2):
+        x = jnp.concatenate(
+            [x_ref[:, m].reshape(2 * FT, FT), x_ref[:, m + 1].reshape(2 * FT, FT)], axis=1
+        )
+        half = dot(f1h[...], x) + dot(f1l[...], x)
+        turned = []
+        for i in range(2):
+            h_re, h_im = half[:FT, i * FT : (i + 1) * FT], half[FT:, i * FT : (i + 1) * FT]
+            turned.append(
+                jnp.concatenate(
+                    [
+                        h_re * tw_re[...] - h_im * tw_im[...],
+                        h_re * tw_im[...] + h_im * tw_re[...],
+                    ],
+                    axis=1,
+                )
+            )
+        turned = jnp.concatenate(turned, axis=0)
+        high = turned.astype(jnp.bfloat16)
+        low = (turned - high.astype(jnp.float32)).astype(jnp.bfloat16)
+        out = dot_nt(f2h[...], high) + dot_nt(f2h[...], low) + dot_nt(f2l[...], high)
+        for i in range(2):
+            rows[pl.ds(m + i, 2 * FT, stride=modes), :] = out[:, i * FT : (i + 1) * FT]
+
+
+def gram_kernel(scale, half_ref, spec_ref, out_ref):
+    sides, parts, _, _, modes, _ = spec_ref.shape
+    row_count = out_ref.shape[2]
+    sources = row_count // modes
+    first = half_ref[0] * sources
+    cols, rows_re, rows_im = [], [], []
+    for side in range(sides):
+        re, im = (spec_ref[side, :, 0, c].reshape(parts * modes, FT) for c in range(2))
+        own = pl.ds(first, sources)
+        own_re, own_im = (spec_ref[side, own, 0, c].reshape(row_count, FT) for c in range(2))
+        cols += [re, im]
+        rows_re += [own_re, own_im]
+        rows_im += [own_im, -own_re]
+    cols = jnp.concatenate(cols, axis=1)
+    rows = jnp.concatenate(
+        [jnp.concatenate(rows_re, axis=1), jnp.concatenate(rows_im, axis=1)], axis=0
+    )
+    lane = lax.broadcasted_iota(jnp.int32, rows.shape, 1)
+    band = (lane % FT) // FB
+    for g in range(FT // FB):
+        kept = jnp.where(band == g, rows, jnp.zeros_like(rows))
+        out = lax.dot_general(
+            kept, cols, (((1,), (1,)), ((), ())), preferred_element_type=jnp.float32
+        )
+        out_ref[g] = (out * scale).reshape(2, row_count, parts * modes)
+
+
+def gram(half, spectra, row_count, scale):
+    sides, parts, high, _, modes, _ = spectra.shape
+    width = parts * modes
+    per = FT // FB
+    return pl.pallas_call(
+        functools.partial(gram_kernel, scale),
+        grid=(high,),
+        out_shape=jax.ShapeDtypeStruct((high * per, 2, row_count, width), jnp.float32),
+        in_specs=[
+            pl.BlockSpec(memory_space=pltpu.SMEM),
+            pl.BlockSpec((sides, parts, 1, 2, modes, FT), lambda j: (0, 0, j, 0, 0, 0)),
+        ],
+        out_specs=pl.BlockSpec((per, 2, row_count, width), lambda j: (j, 0, 0, 0)),
+        compiler_params=pltpu.CompilerParams(vmem_limit_bytes=BIG),
+    )(half, spectra)
+
+
+def tiled_shards(input_field, kerr_coeff, block_list):
+    parts, sides = lax.axis_size("mode"), lax.axis_size("real")
+    _, _, modes, times = input_field.shape
+    width = parts * modes
+    coef = kerr_coeff[0].reshape(MB, MB, MB * MB).transpose(1, 0, 2).reshape(MB * MB, MB * MB)
+    listed = jnp.pad(block_list, ((0, 7), (0, FT - block_list.shape[1])))
+    spectra = spectra_of(input_field.reshape(2, modes, times), coef, listed, parts, sides)
+    half = lax.axis_index("real").astype(jnp.int32).reshape(1)
+    return gram(half, spectra, width // sides, 1.0 / (FB * sides))
+
+
+def tiles_fit(mesh):
+    parts = mesh.shape["mode"]
+    return FT % parts == 0 and (2 * FT // parts) % 16 == 0 and mesh.shape["real"] <= 2
+
+
+def either(mesh, input_field, kerr_coeff, block_list):
+    modes = input_field.shape[2]
+    blocks_each = kerr_coeff.shape[0]
+    fits = tiles_fit(mesh) and modes % 16 == 0 and blocks_each == 1
+    fits = fits and input_field.shape[1] == 1 and input_field.shape[3] == NT
+    return (tiled_shards if fits else shards)(input_field, kerr_coeff, block_list)
+
+
 def solution(mesh):
     return jax.shard_map(
-        shards,
+        functools.partial(either, mesh),
         mesh=mesh,
         in_specs=(P(None, "real", "mode", None), P("mode", None, None), P("mode", None)),
         out_specs=P("mode", None, "real", None),

time: 300 us -> 105 us (0.35)
  blocking collectives: 111 us -> 0 us
  local copies, waits for them, and re-layouts: 106 us -> 2.58 us
  Pallas kernels: 0 us -> 102 us
  waiting for transfers between devices: 23.6 us -> 0 us
  matrix products: 18.1 us -> 0 us
  between operations: 13.7 us -> 0.01 us
  starting transfers between devices: 12.3 us -> 0 us
  other arithmetic: 11.5 us -> 0 us
    pallas_call x0 -> x2, Pallas kernels: none -> 102 us  [the longest x1 93.6 us: spectra_of(): pl.pallas_call(functools.partial(whole_kernel, parts, sides), out_shape=j...]
    all_gather x2 -> x0, blocking collectives: 89.6 us -> none  [the longest x1 50.9 us: shards(): block_piece = lax.all_gather(block_list, 'mode', axis=0, tiled=True)]
    unnamed x12 -> x0, local copies, waits for them, and re-layouts: 34.7 us -> none
    all_to_all x5 -> x0, local copies, waits for them, and re-layouts: 31.3 us -> none  [the longest x2 30.4 us: shards(): lax.all_to_all(input_field, 'mode', split_axis=3, concat_axis=2, tiled=True)]
    all_to_all x1 -> x0, blocking collectives: 21.6 us -> none  [shards(): lax.all_to_all(spectrum, 'mode', split_axis=3, concat_axis=2, tiled=True)]
    dot_general x17 -> x0, matrix products: 18.1 us -> none  [the longest x4 4.74 us: second_pass(): jnp.einsum('jn,rmkn->rmjk', table, data, precision=lax.Precision.HIGH)]
    all_to_all x2 -> x0, waiting for transfers between devices: 14.6 us -> none  [the longest x1 14.6 us: shards(): lax.all_to_all(stepped, 'mode', split_axis=2, concat_axis=3, tiled=True)]
    all_to_all x2 -> x0, starting transfers between devices: 12.1 us -> none  [the longest x1 8.47 us: shards(): lax.all_to_all(input_field, 'mode', split_axis=3, concat_axis=2, tiled=True)]
  transfers between devices with their start and end apart: 3 -> 0, of which waited for: 2 -> 0; matrix products, arithmetic and copies ran while one was open for 0% -> 0% of each run, Pallas kernels for 0% -> 0%
where the time goes in v2:
time: 105 us; the launch traced here: 104 us
  Pallas kernels  102 us (97%)
  local copies, waits for them, and re-layouts  2.58 us (2%)
    pallas_call x1, Pallas kernels, spectra_of(): pl.pallas_call(functools.partial(whole_kernel, parts, sides), out_shape=j...  93.6 us
    pallas_call x1, Pallas kernels, gram(): pl.pallas_call(functools.partial(gram_kernel, scale), grid=(high,), out_s...  8.31 us

profile of v2, /device:TPU:0, one launch (start us, length us, event | category | flops | bytes accessed | tf_op | source)
XLA Modules:
  0.0 104.5 jit_solution(10950021622586678436)
XLA Ops:
  0.0 1.3 %pad.4.list_ref = s32[8,128]{1,0:T(8,128)} pad(s32[1,4]{1,0:T(1,128)} %param.11, s32[]{:T(128)} %constant.7.clone.1), padding=0_7x0_124 | pad | bytes 4116 | tf_op jit(solution)/shard_map/jit(_pad)/pad | solution.py:463
  1.3 1.3 %copy.12 = bf16[8,8,64]{2,0,1:T(8,128)(2,1)} copy(bf16[8,8,64]{2,1,0:T(8,128)(2,1)} %bitcast.10) | data formatting | bytes 16384 | tf_op jit(solution)/shard_map/reshape;squeeze | solution.py:462
  2.6 93.6 %shard_map.91.spec_ref = bf16[2,16,8,2,16,128]{5,4,3,2,1,0:T(8,128)(2,1)} custom-call(bf16[2,16,16384]{2,1,0:T(8,128)(2,1)} %bitcast.8, bf16[64,64]{1,0:T(8,128)(2,1)} %bitcast.9, s32[8,128]{1,0:T(8,128)} %pad.4.list_ref, bf16[256,256]{1,0:T(8,128)(2,1)} %constant.18.clone.f1h, bf16[256,256]{1,0:T(8,128)(2,1)} %constant.19.clone.f1l, ...), custom_call_target="tpu_custom_call" | custom-call | tf_op jit(solution)/shard_map/pallas_call | solution.py:334
  96.2 8.3 %shard_map.92 = f32[32,2,128,256]{3,2,1,0:T(8,128)} custom-call(s32[1]{0:T(128)} %bitcast.half_ref, bf16[2,16,8,2,16,128]{5,4,3,2,1,0:T(8,128)(2,1)} %shard_map.91.spec_ref), custom_call_target="tpu_custom_call" | custom-call | tf_op jit(solution)/shard_map/pallas_call | solution.py:445

commit v3 on v2

--- a/solution.py
+++ b/solution.py
@@ -186,7 +186,7 @@
 
 
 def whole_kernel(parts, sides, x_ref, coef_ref, list_ref, f1h, f1l, tw_re, tw_im, f2h, f2l,
-                 out_ref, timed, coefs, lists, list_s, fld, terms, rows, stepped, by_mode, spec,
+                 out_ref, timed, coefs, swapped, lists, list_s, fld, terms, rows, stepped, by_mode, spec,
                  sends, recvs, own_sems):
     me = lax.axis_index("mode")
     other = {"real": 1 - lax.axis_index("real")}
@@ -195,7 +195,8 @@
     width = parts * modes
     groups = width // MB
     fine = steps // FT
-    half = steps // 2
+    pieces = min(4, fine)
+    half = steps // pieces
     piece = min(half, 256)
     order = step_order(parts)
     barrier = pltpu.get_barrier_semaphore()
@@ -213,43 +214,48 @@
     def landing(part):
         return timed.at[me, :, :, pl.ds(part * half, half)]
 
-    small, first, later = [], [], []
+    small, field_copies = [], [[] for _ in range(pieces)]
     for step in order:
         to = lax.rem(me + step, parts)
         there = {"mode": to}
         small.append(remote(coef_ref, coefs.at[me], sends.at[0, step], recvs.at[0, step], there))
         small.append(remote(list_ref, lists.at[me], sends.at[1, step], recvs.at[1, step], there))
-    for part, copies in ((0, first), (1, later)):
+    for part, copies in enumerate(field_copies):
         for step in order:
             to = lax.rem(me + step, parts)
             copies.append(
                 remote(
                     chunk(to, part),
                     landing(part),
-                    sends.at[2 + part, step],
-                    recvs.at[2 + part, step],
+                    sends.at[4 + part, step],
+                    recvs.at[4 + part, step],
                     {"mode": to},
                 )
             )
-    for slot, (here, there) in enumerate(
-        (
-            (coef_ref, coefs.at[me]),
-            (list_ref, lists.at[me]),
-            (chunk(me, 0), landing(0)),
-            (chunk(me, 1), landing(1)),
-        )
-    ):
+    for slot, (here, there) in enumerate(((coef_ref, coefs.at[me]), (list_ref, lists.at[me]))):
         copy = pltpu.make_async_copy(here, there, own_sems.at[slot])
         copy.start()
-        (small, small, first, later)[slot].append(copy)
+        small.append(copy)
+    for part, copies in enumerate(field_copies):
+        copy = pltpu.make_async_copy(chunk(me, part), landing(part), own_sems.at[4 + part])
+        copy.start()
+        copies.append(copy)
     for copy in small:
         copy.wait()
-    copy = pltpu.make_async_copy(lists, list_s, own_sems.at[4])
+    copy = pltpu.make_async_copy(lists, list_s, own_sems.at[2])
     copy.start()
     copy.wait()
     blocks = coefs.shape[0]
     owners = owner_table(blocks, width, list_s)
-    for part, copies in ((0, first), (1, later)):
+    order_of = (MB * MB, MB * MB)
+    row = lax.broadcasted_iota(jnp.int32, order_of, 0)
+    col = lax.broadcasted_iota(jnp.int32, order_of, 1)
+    swap = (col == (row % MB) * MB + row // MB).astype(jnp.float32).astype(jnp.bfloat16)
+    for k in range(blocks):
+        swapped[k] = jnp.dot(
+            swap, coefs[k], preferred_element_type=jnp.float32
+        ).astype(jnp.bfloat16)
+    for part, copies in enumerate(field_copies):
         for copy in copies:
             copy.wait()
         span = pl.ds(part * half, half)
@@ -257,7 +263,7 @@
             fld[c, :, :, span] = timed[:, c, :, span].astype(jnp.float32).reshape(groups, MB, half)
 
         def one_block(k, carry):
-            coef = coefs[k]
+            coef = swapped[k]
             for at in range(part * half, (part + 1) * half, piece):
                 kerr_terms_at(at, piece, k, list_s, coef, fld, terms)
             return carry
@@ -279,18 +285,33 @@
                     ]
     stepped[...] = rows[...].astype(jnp.bfloat16).reshape(stepped.shape)
 
-    pending = []
-    for step in order:
-        to = lax.rem(me + step, parts)
-        pending.append(
-            remote(stepped.at[to], by_mode.at[me], sends.at[4, step], recvs.at[4, step], {"mode": to})
+    quarters = min(4, modes // 2)
+    few = modes // quarters
+    mode_copies = []
+    for part in range(quarters):
+        some = pl.ds(part * few, few)
+        copies = []
+        for step in order:
+            to = lax.rem(me + step, parts)
+            copies.append(
+                remote(
+                    stepped.at[to, some],
+                    by_mode.at[me, some],
+                    sends.at[8 + part, step],
+                    recvs.at[8 + part, step],
+                    {"mode": to},
+                )
+            )
+        copy = pltpu.make_async_copy(
+            stepped.at[me, some], by_mode.at[me, some], own_sems.at[8 + part]
         )
-    copy = pltpu.make_async_copy(stepped.at[me], by_mode.at[me], own_sems.at[5])
-    copy.start()
-    for copy in pending + [copy]:
-        copy.wait()
-
-    dft_kernel(by_mode, f1h, f1l, tw_re, tw_im, f2h, f2l, rows)
+        copy.start()
+        mode_copies.append(copies + [copy])
+    for part, copies in enumerate(mode_copies):
+        for copy in copies:
+            copy.wait()
+        some = range(part * few, (part + 1) * few)
+        dft_modes(some, by_mode, f1h, f1l, tw_re, tw_im, f2h, f2l, rows)
     spec[...] = rows[...].astype(jnp.bfloat16).reshape(spec.shape)
 
     pending, passed = [], []
@@ -298,14 +319,14 @@
         to = lax.rem(me + step, parts)
         pending.append(
             (
-                remote(spec.at[to], out_ref.at[0, me], sends.at[5, step], recvs.at[5, step], {"mode": to}),
+                remote(spec.at[to], out_ref.at[0, me], sends.at[2, step], recvs.at[2, step], {"mode": to}),
                 lax.rem(me - step + parts, parts),
             )
         )
-    copy = pltpu.make_async_copy(spec.at[me], out_ref.at[0, me], own_sems.at[6])
+    copy = pltpu.make_async_copy(spec.at[me], out_ref.at[0, me], own_sems.at[3])
     copy.start()
     if sides > 1:
-        passed.append(remote(spec.at[me], out_ref.at[1, me], sends.at[6, 0], recvs.at[6, 0], other))
+        passed.append(remote(spec.at[me], out_ref.at[1, me], sends.at[3, 0], recvs.at[3, 0], other))
     for step, (arrival, source) in zip(order, pending):
         arrival.wait_recv()
         if sides > 1:
@@ -313,8 +334,8 @@
                 remote(
                     out_ref.at[0, source],
                     out_ref.at[1, source],
-                    sends.at[6, step],
-                    recvs.at[6, step],
+                    sends.at[3, step],
+                    recvs.at[3, step],
                     other,
                 )
             )
@@ -334,10 +355,11 @@
     return pl.pallas_call(
         functools.partial(whole_kernel, parts, sides),
         out_shape=jax.ShapeDtypeStruct((sides, parts, fine, 2, modes, FT), half),
-        in_specs=[pl.BlockSpec(memory_space=VMEM)] * 9,
+        in_specs=[pl.BlockSpec(memory_space=pl.ANY)] + [pl.BlockSpec(memory_space=VMEM)] * 8,
         out_specs=pl.BlockSpec(memory_space=VMEM),
         scratch_shapes=[
             VMEM((parts, 2, modes, steps), half),
+            VMEM((parts,) + coef.shape, half),
             VMEM((parts,) + coef.shape, half),
             VMEM((parts,) + listed.shape, jnp.int32),
             pltpu.SMEM((parts,) + listed.shape, jnp.int32),
@@ -347,9 +369,9 @@
             VMEM((parts, modes, 2 * fine, FT), half),
             VMEM((parts, modes, 2 * fine, FT), half),
             VMEM((parts, fine, 2, modes, FT), half),
-            pltpu.SemaphoreType.DMA((7, parts)),
-            pltpu.SemaphoreType.DMA((7, parts)),
-            pltpu.SemaphoreType.DMA((7,)),
+            pltpu.SemaphoreType.DMA((12, parts)),
+            pltpu.SemaphoreType.DMA((12, parts)),
+            pltpu.SemaphoreType.DMA((12,)),
         ],
         compiler_params=pltpu.CompilerParams(
             collective_id=0, has_side_effects=True, vmem_limit_bytes=BIG
@@ -379,14 +401,14 @@
     )
 
 
-def dft_kernel(x_ref, f1h, f1l, tw_re, tw_im, f2h, f2l, rows):
+def dft_modes(some, x_ref, f1h, f1l, tw_re, tw_im, f2h, f2l, rows):
     modes = x_ref.shape[1]
     nt = (((1,), (1,)), ((), ()))
     dot = functools.partial(jnp.dot, preferred_element_type=jnp.float32)
     dot_nt = functools.partial(
         lax.dot_general, dimension_numbers=nt, preferred_element_type=jnp.float32
     )
-    for m in range(0, modes, 2):
+    for m in some[::2]:
         x = jnp.concatenate(
             [x_ref[:, m].reshape(2 * FT, FT), x_ref[:, m + 1].reshape(2 * FT, FT)], axis=1
         )
@@ -459,9 +481,9 @@
     parts, sides = lax.axis_size("mode"), lax.axis_size("real")
     _, _, modes, times = input_field.shape
     width = parts * modes
-    coef = kerr_coeff[0].reshape(MB, MB, MB * MB).transpose(1, 0, 2).reshape(MB * MB, MB * MB)
-    listed = jnp.pad(block_list, ((0, 7), (0, FT - block_list.shape[1])))
-    spectra = spectra_of(input_field.reshape(2, modes, times), coef, listed, parts, sides)
+    spectra = spectra_of(
+        input_field.reshape(2, modes, times), kerr_coeff[0], block_list, parts, sides
+    )
     half = lax.axis_index("real").astype(jnp.int32).reshape(1)
     return gram(half, spectra, width // sides, 1.0 / (FB * sides))
 

time: 105 us -> 105 us (level)
  local copies, waits for them, and re-layouts: 2.58 us -> 0 us
  Pallas kernels: 102 us -> 104 us
    pallas_call x1, Pallas kernels: 93.6 us -> 95.5 us  [spectra_of(): pl.pallas_call(functools.partial(whole_kernel, parts, sides), out_shape=j...]
    another operation x1 -> x0, local copies, waits for them, and re-layouts: 1.33 us -> none  [tiled_shards(): kerr_coeff[0].reshape(MB, MB, MB * MB).transpose(1, 0, 2)]
    pad x1 -> x0, local copies, waits for them, and re-layouts: 1.25 us -> none  [tiled_shards(): listed = jnp.pad(block_list, ((0, 7), (0, FT - block_list.shape[1])))]
where the time goes in v3:
time: 105 us; the launch traced here: 104 us
  Pallas kernels  104 us (99%)
    pallas_call x1, Pallas kernels, spectra_of(): pl.pallas_call(functools.partial(whole_kernel, parts, sides), out_shape=j...  95.5 us
    pallas_call x1, Pallas kernels, gram(): pl.pallas_call(functools.partial(gram_kernel, scale), grid=(high,), out_s...  8.31 us

profile of v3, /device:TPU:0, one launch (start us, length us, event | category | flops | bytes accessed | tf_op | source)
XLA Modules:
  0.0 103.9 jit_solution(8985225536586568794)
XLA Ops:
  0.0 95.5 %shard_map.91.spec_ref = bf16[2,16,8,2,16,128]{5,4,3,2,1,0:T(8,128)(2,1)} custom-call(bf16[2,16,16384]{2,1,0:T(8,128)(2,1)} %bitcast.3, bf16[64,64]{1,0:T(8,128)(2,1)} %bitcast.4, s32[1,4]{1,0:T(1,128)} %list_ref.1, bf16[256,256]{1,0:T(8,128)(2,1)} %constant.16.clone.f1h, bf16[256,256]{1,0:T(8,128)(2,1)} %constant.17.clone.f1l, ...), custom_call_target="tpu_custom_call" | custom-call | tf_op jit(solution)/shard_map/pallas_call | solution.py:355
  95.5 8.3 %shard_map.92 = f32[32,2,128,256]{3,2,1,0:T(8,128)} custom-call(s32[1]{0:T(128)} %bitcast.half_ref, bf16[2,16,8,2,16,128]{5,4,3,2,1,0:T(8,128)(2,1)} %shard_map.91.spec_ref), custom_call_target="tpu_custom_call" | custom-call | tf_op jit(solution)/shard_map/pallas_call | solution.py:467

commit v4 on v3

--- a/solution.py
+++ b/solution.py
@@ -90,11 +90,11 @@
 
 
 def gram_parts(rows_part, cols_part):
-    quarters = jnp.einsum(
+    mode_parts = jnp.einsum(
         "crpbf,drqbf->bcdpq", rows_part, cols_part, preferred_element_type=jnp.float32
     )
     return jnp.stack(
-        [quarters[:, 0, 0] + quarters[:, 1, 1], quarters[:, 1, 0] - quarters[:, 0, 1]], axis=1
+        [mode_parts[:, 0, 0] + mode_parts[:, 1, 1], mode_parts[:, 1, 0] - mode_parts[:, 0, 1]], axis=1
     )
 
 
@@ -195,7 +195,7 @@
     width = parts * modes
     groups = width // MB
     fine = steps // FT
-    pieces = min(4, fine)
+    pieces = min(2, fine)
     half = steps // pieces
     piece = min(half, 256)
     order = step_order(parts)
@@ -285,10 +285,10 @@
                     ]
     stepped[...] = rows[...].astype(jnp.bfloat16).reshape(stepped.shape)
 
-    quarters = min(4, modes // 2)
-    few = modes // quarters
+    mode_parts = min(2, modes // 2)
+    few = modes // mode_parts
     mode_copies = []
-    for part in range(quarters):
+    for part in range(mode_parts):
         some = pl.ds(part * few, few)
         copies = []
         for step in order:

time: 105 us -> 102 us (0.971); the launches traced: 104 us -> 102 us
  Pallas kernels: 104 us -> 102 us
    pallas_call x1, Pallas kernels: 95.5 us -> 93.9 us  [spectra_of(): pl.pallas_call(functools.partial(whole_kernel, parts, sides), out_shape=j...]
where the time goes in v4:
time: 102 us
  Pallas kernels  102 us (100%)
    pallas_call x1, Pallas kernels, spectra_of(): pl.pallas_call(functools.partial(whole_kernel, parts, sides), out_shape=j...  93.9 us
    pallas_call x1, Pallas kernels, gram(): pl.pallas_call(functools.partial(gram_kernel, scale), grid=(high,), out_s...  8.3 us

profile of v4, /device:TPU:0, one launch (start us, length us, event | category | flops | bytes accessed | tf_op | source)
XLA Modules:
  0.0 102.2 jit_solution(1047885474980523863)
XLA Ops:
  0.0 93.9 %shard_map.91.spec_ref = bf16[2,16,8,2,16,128]{5,4,3,2,1,0:T(8,128)(2,1)} custom-call(bf16[2,16,16384]{2,1,0:T(8,128)(2,1)} %bitcast.3, bf16[64,64]{1,0:T(8,128)(2,1)} %bitcast.4, s32[1,4]{1,0:T(1,128)} %list_ref.1, bf16[256,256]{1,0:T(8,128)(2,1)} %constant.16.clone.f1h, bf16[256,256]{1,0:T(8,128)(2,1)} %constant.17.clone.f1l, ...), custom_call_target="tpu_custom_call" | custom-call | tf_op jit(solution)/shard_map/pallas_call | solution.py:355
  93.9 8.3 %shard_map.92 = f32[32,2,128,256]{3,2,1,0:T(8,128)} custom-call(s32[1]{0:T(128)} %bitcast.half_ref, bf16[2,16,8,2,16,128]{5,4,3,2,1,0:T(8,128)(2,1)} %shard_map.91.spec_ref), custom_call_target="tpu_custom_call" | custom-call | tf_op jit(solution)/shard_map/pallas_call | solution.py:467

commit v5 on v4

--- a/solution.py
+++ b/solution.py
@@ -268,7 +268,7 @@
                 kerr_terms_at(at, piece, k, list_s, coef, fld, terms)
             return carry
 
-        lax.fori_loop(0, blocks, one_block, 0)
+        lax.fori_loop(0, blocks, one_block, 0, unroll=2)
         for c in range(2):
             term = terms[1 - c, :, span]
             high = term.astype(jnp.bfloat16)

time: 102 us -> 101 us (level)
    pallas_call x1, Pallas kernels: 93.9 us -> 92.8 us  [spectra_of(): pl.pallas_call(functools.partial(whole_kernel, parts, sides), out_shape=j...]
where the time goes in v5:
time: 101 us
  Pallas kernels  101 us (100%)
    pallas_call x1, Pallas kernels, spectra_of(): pl.pallas_call(functools.partial(whole_kernel, parts, sides), out_shape=j...  92.8 us
    pallas_call x1, Pallas kernels, gram(): pl.pallas_call(functools.partial(gram_kernel, scale), grid=(high,), out_s...  8.32 us

profile of v5, /device:TPU:0, one launch (start us, length us, event | category | flops | bytes accessed | tf_op | source)
XLA Modules:
  0.0 101.1 jit_solution(1837882840755797653)
XLA Ops:
  0.0 92.8 %shard_map.91.spec_ref = bf16[2,16,8,2,16,128]{5,4,3,2,1,0:T(8,128)(2,1)} custom-call(bf16[2,16,16384]{2,1,0:T(8,128)(2,1)} %bitcast.3, bf16[64,64]{1,0:T(8,128)(2,1)} %bitcast.4, s32[1,4]{1,0:T(1,128)} %list_ref.1, bf16[256,256]{1,0:T(8,128)(2,1)} %constant.16.clone.f1h, bf16[256,256]{1,0:T(8,128)(2,1)} %constant.17.clone.f1l, ...), custom_call_target="tpu_custom_call" | custom-call | tf_op jit(solution)/shard_map/pallas_call | solution.py:355
  92.8 8.3 %shard_map.92 = f32[32,2,128,256]{3,2,1,0:T(8,128)} custom-call(s32[1]{0:T(128)} %bitcast.half_ref, bf16[2,16,8,2,16,128]{5,4,3,2,1,0:T(8,128)(2,1)} %shard_map.91.spec_ref), custom_call_target="tpu_custom_call" | custom-call | tf_op jit(solution)/shard_map/pallas_call | solution.py:467
